TPU v7x, 128 devices: a whole 4x4x4 slice. The times are simulated.
128 devices in a mesh: tm: 64 (over x, z, y), row: 2 (over core).
Axes of the slice: x: 4, y: 4, z: 4, core: 2. Of those that a mesh axis runs over, the one named last changes fastest.
Arguments:
- init_mean: float32 [1024], replicated, may hold values from -6 to 6
- jac_skew: bfloat16 [128, 1024, 1024], P('tm', 'row'), may hold values from -0.1875 to 0.1875
- gain_diag: float32 [1024], replicated, may hold values from 0.3 to 0.9
- gain_cross: float32 [1024, 1024], replicated, may hold values from -0.0234375 to 0.0234375
- smooth_diag: float32 [1024], replicated, may hold values from 0.2 to 0.8
- smooth_cross: float32 [1024, 1024], replicated, may hold values from -0.046875 to 0.046875
- obs_values: float32 [128, 128], P(('tm', 'row')), may hold values from -6 to 6
- obs_prec: float32 [128], P(('tm', 'row')), may hold values from 0.2 to 2
- obs_sensor: int32 [128], P(('tm', 'row')), may hold values from 0 to 511
- obs_block: int32 [128], P(('tm', 'row')), may hold values from 0 to 7
- sensor_step: int32 [512], replicated, may hold values from 0 to 127
Outputs:
- filtered: float32 [128, 1024], P('tm', 'row')
- smoothed: float32 [128, 1024], P('tm', 'row')
All inputs are finite; a program needn't handle non-finite values.
Results may differ from a plain program's by a relative error of at most 0.0003.
Values may be sent and summed in bfloat16 or wider, within the bound.
A program may use at most 128 MiB of HBM per device.

v0:
```python
import jax
import jax.numpy as jnp
from jax import lax
from jax.sharding import PartitionSpec as P

step_length = 0.25
finest_accuracy = lax.Precision.HIGHEST


def shifted(block, axis, distance):
    devices = range(lax.axis_size(axis))
    route = [(i - distance, i) for i in devices if i - distance in devices]
    return lax.ppermute(block, axis, route)


def shards(
    init_mean,
    jac_skew,
    gain_diag,
    gain_cross,
    smooth_diag,
    smooth_cross,
    obs_values,
    obs_prec,
    obs_sensor,
    obs_block,
    sensor_step,
):
    row_total = lax.axis_size("row")
    row_index = lax.axis_index("row")
    local_steps = jac_skew.shape[0]
    half_rows = jac_skew.shape[1]
    width = jac_skew.shape[2]
    block_width = obs_values.shape[1]
    block_total = width // block_width
    first_row = row_index * half_rows
    sensor_hits = obs_sensor[:, None] == jnp.arange(sensor_step.shape[0], dtype=jnp.int32)[None, :]
    obs_steps = jnp.sum(jnp.where(sensor_hits, sensor_step[None, :], 0), axis=1)
    block_hits = (obs_block[:, None] == jnp.arange(block_total, dtype=jnp.int32)[None, :]).astype(
        jnp.float32
    )
    weighted = obs_prec[:, None] * obs_values
    value_full = (block_hits[:, :, None] * weighted[:, None, :]).reshape(-1, width)
    weight_full = jnp.broadcast_to(
        block_hits[:, :, None] * obs_prec[:, None, None],
        (obs_values.shape[0], block_total, block_width),
    ).reshape(-1, width)
    half_terms = [
        jnp.concatenate(
            [
                value_full[:, half_index * half_rows : (half_index + 1) * half_rows],
                weight_full[:, half_index * half_rows : (half_index + 1) * half_rows],
            ],
            axis=1,
        )
        for half_index in range(row_total)
    ]
    row_ids = jnp.arange(local_steps * lax.axis_size(("tm", "row")), dtype=jnp.int32)
    device_ids = row_ids // local_steps
    step_ids = device_ids // row_total * local_steps + row_ids % local_steps
    half_ids = device_ids % row_total
    step_match = obs_steps[:, None] == step_ids[None, :]
    term_sum = jnp.zeros((local_steps * lax.axis_size(("tm", "row")), 2 * half_rows), jnp.float32)
    for half_index in range(row_total):
        selector = (step_match & (half_ids == half_index)[None, :]).astype(jnp.float32)
        term_sum = term_sum + jnp.dot(
            selector.T,
            half_terms[half_index],
            precision=finest_accuracy,
            preferred_element_type=jnp.float32,
        )
    observed = lax.psum_scatter(term_sum, ("tm", "row"), scatter_dimension=0, tiled=True)
    halves = lax.all_gather(observed, "row", axis=1, tiled=True).reshape(
        local_steps, row_total, 2, half_rows
    )
    value_sums = halves[:, :, 0, :].reshape(local_steps, width)
    weight_sums = halves[:, :, 1, :].reshape(local_steps, width)
    measured_share = weight_sums / (weight_sums + 1.0)
    goal_estimate = value_sums / (weight_sums + 1.0)
    skew_full = lax.all_gather(jac_skew, "row", axis=1, tiled=True).astype(jnp.float32)
    jacobian = skew_full - jnp.swapaxes(skew_full, 1, 2)
    identity_rows = (
        jnp.arange(half_rows, dtype=jnp.int32)[:, None] + first_row
        == jnp.arange(width, dtype=jnp.int32)[None, :]
    ).astype(jnp.float32)
    jacobian_rows = lax.dynamic_slice_in_dim(jacobian, first_row, half_rows, 1)
    section = identity_rows + step_length / 4.0 * jacobian_rows
    for divisor in (3.0, 2.0):
        section = identity_rows + step_length / divisor * jnp.einsum(
            "shk,skd->shd", section, jacobian, precision=finest_accuracy
        )
    tangent_part = identity_rows + step_length * jnp.einsum(
        "shk,skd->shd", section, jacobian, precision=finest_accuracy
    )
    jacobian_propagator = lax.all_gather(tangent_part, "row", axis=1, tiled=True)
    entire_blend_matrix = gain_cross + jnp.diag(gain_diag)

    def filter_steps(start_mean):
        present_estimate = start_mean
        mean_list = []
        increment_list = []
        for interval_length in range(local_steps):
            predicted_estimate = jnp.dot(
                jacobian_propagator[interval_length], present_estimate, precision=finest_accuracy
            )
            update_correction = jnp.dot(
                entire_blend_matrix,
                goal_estimate[interval_length]
                - measured_share[interval_length] * predicted_estimate,
                precision=finest_accuracy,
            )
            present_estimate = predicted_estimate + update_correction
            mean_list.append(present_estimate)
            increment_list.append(update_correction)
        return (jnp.stack(mean_list), jnp.stack(increment_list))

    gain_part = lax.dynamic_slice_in_dim(entire_blend_matrix, first_row, half_rows, 0)
    map_parts = []
    for interval_length in range(local_steps):
        scaled = measured_share[interval_length][:, None] * jacobian_propagator[interval_length]
        own_rows = lax.dynamic_slice_in_dim(
            jacobian_propagator[interval_length], first_row, half_rows, 0
        )
        map_parts.append(own_rows - jnp.dot(gain_part, scaled, precision=finest_accuracy))
    earlier_maps = lax.all_gather(
        jnp.stack(map_parts[: local_steps - 1]), "row", axis=1, tiled=True
    )
    composed = map_parts[local_steps - 1]
    interval_length = 0
    composed = jnp.dot(composed, earlier_maps[interval_length], precision=finest_accuracy)
    composite = lax.all_gather(composed, "row", axis=0, tiled=True)
    zero_vector = jnp.zeros((width,), jnp.float32)
    offset = filter_steps(zero_vector)[0][local_steps - 1]
    tm_index = lax.axis_index("tm")

    def chain_turn(turn_index, incoming):
        outgoing = jnp.dot(composite, incoming, precision=finest_accuracy) + offset
        arrived = shifted(outgoing, "tm", 1)
        return jnp.where(tm_index == 0, init_mean, arrived)

    start_mean = lax.fori_loop(0, lax.axis_size("tm") - 1, chain_turn, init_mean)
    filtered, increments = filter_steps(start_mean)
    later_incs = shifted(increments, "tm", -1)
    window = jnp.concatenate([increments, later_incs], axis=0)
    smoother_gain = smooth_cross + jnp.diag(smooth_diag)
    carried = jnp.zeros((local_steps, width), jnp.float32)
    for lag_steps in range(local_steps, 0, -1):
        carried = window[lag_steps : lag_steps + local_steps] + jnp.dot(
            carried, smoother_gain.T, precision=finest_accuracy
        )
    smoothed = filtered + jnp.dot(carried, smoother_gain.T, precision=finest_accuracy)
    filtered_part = lax.dynamic_slice_in_dim(filtered, first_row, half_rows, 1)
    smoothed_part = lax.dynamic_slice_in_dim(smoothed, first_row, half_rows, 1)
    return (filtered_part, smoothed_part)


def solution(mesh):
    in_specs = (
        P(),
        P("tm", "row", None),
        P(),
        P(),
        P(),
        P(),
        P(("tm", "row"), None),
        P(("tm", "row")),
        P(("tm", "row")),
        P(("tm", "row")),
        P(),
    )
    out_specs = (P("tm", "row"), P("tm", "row"))
    return jax.shard_map(shards, mesh=mesh, in_specs=in_specs, out_specs=out_specs, check_vma=False)
```

profile of v0, /device:TPU:2, one launch (start us, length us, event | category | flops | bytes accessed | tf_op | source)
XLA Modules:
  0.0 1251.3 jit_solution(18019109508423364695)
XLA Ops:
  17.0 14.0 %all-gather.6.cloned.1.call-done = bf16[2,1024,1024]{1,2,0:T(8,128)(2,1)} async-done(((bf16[2,512,1024]{1,2,0:T(8,128)(2,1)}), bf16[2,1024,1024]{1,2,0:T(8,128)(2,1)}) %all-gather.6.cloned.1.call-update) | async-done | bytes 4194320 | tf_op jit(solution)/shard_map/all_gather | solution.py:80
  44.0 14.3 %fusion.16 = f32[2,512,1024]{2,1,0:T(8,128)S(1)} fusion(f32[2,1024,1024]{2,1,0:T(8,128)S(1)} %bitcast_subtract_fusion, s32[]{:T(128)S(6)} %select_n.82, f32[512,1024]{1,0:T(8,128)S(1)} %fusion.41), kind=kOutput, calls=%fused_computation.24 | convolution fusion | flops 12886999040 | bytes 18874372 | tf_op jit(solution)/shard_map/shk,skd->shd/dot_general | solution.py:89
  58.3 15.1 %fusion.13 = f32[2,512,1024]{2,1,0:T(8,128)} fusion(f32[2,1024,1024]{2,1,0:T(8,128)S(1)} %bitcast_subtract_fusion, f32[2,512,1024]{2,1,0:T(8,128)S(1)} %fusion.16, f32[512,1024]{1,0:T(8,128)S(1)} %fusion.41), kind=kOutput, calls=%fused_computation.21 | convolution fusion | flops 12886999040 | bytes 18874368 | tf_op jit(solution)/shard_map/shk,skd->shd/dot_general | solution.py:89
  73.4 16.8 %multiply_add_fusion = f32[2,512,1024]{2,1,0:T(8,128)} fusion(f32[2,1024,1024]{2,1,0:T(8,128)S(1)} %bitcast_subtract_fusion, f32[2,512,1024]{2,1,0:T(8,128)} %fusion.13, f32[512,1024]{1,0:T(8,128)S(1)} %fusion.41), kind=kOutput, calls=%fused_computation.17 | convolution fusion | flops 12889096192 | bytes 18874368 | tf_op jit(solution)/shard_map/shk,skd->shd/dot_general | solution.py:92
  95.7 70.9 %all-reduce.3.cloned.1.call-done = f32[256,1024]{1,0:T(8,128)} async-done(((f32[256,1024]{1,0:T(8,128)}), f32[256,1024]{1,0:T(8,128)}) %all-reduce.3.cloned.1.call-update) | async-done | bytes 1048592
  176.4 8.6 bitcast_subtract_fusion.1
  185.4 9.9 fusion.4
  200.9 10.8 fusion.25
  231.4 975.9 %while.12 = (s32[]{:T(128)}, f32[1024]{0:T(1024)S(1)}, pred[]{:T(512)}, f32[1024,1024]{1,0:T(8,128)}, f32[1024]{0:T(1024)S(1)}, /*index=5*/f32[1024]{0:T(1024)S(1)}, s32[]{:T(128)}) while((s32[]{:T(128)}, f32[1024]{0:T(1024)S(1)}, pred[]{:T(512)}, f32[1024,1024]{1,0:T(8,128)}, f32[1024]{0:T(1024)S(1)}, /*index=5*/f32[1024]{0:T(1024)S(1)}, ...), condition=%wide.region_3.4_spmd, body=%wide.region_2.3_spmd.sunk | while | flops 12584962 | bytes 4243574 | solution.py:141
  254.7 7.8 collective-permute-done
  270.2 7.8 collective-permute-done
  285.7 7.8 collective-permute-done
  301.2 7.8 collective-permute-done
  332.2 7.8 collective-permute-done
  347.7 7.8 collective-permute-done
  363.2 7.8 collective-permute-done
  378.6 7.8 collective-permute-done
  394.1 7.8 collective-permute-done
  409.6 7.8 collective-permute-done
  425.1 7.8 collective-permute-done
  440.6 7.8 collective-permute-done
  456.1 7.8 collective-permute-done
  471.6 7.8 collective-permute-done
  487.1 7.8 collective-permute-done
  502.6 7.8 collective-permute-done
  518.0 7.8 collective-permute-done
  533.5 7.8 collective-permute-done
  549.0 7.8 collective-permute-done
  564.5 7.8 collective-permute-done
  580.0 7.8 collective-permute-done
  595.5 7.8 collective-permute-done
  626.5 7.8 collective-permute-done
  641.9 7.8 collective-permute-done
  657.4 7.8 collective-permute-done
  672.9 7.8 collective-permute-done
  688.4 7.8 collective-permute-done
  703.9 7.8 collective-permute-done
  719.4 7.8 collective-permute-done
  734.9 7.8 collective-permute-done
  750.4 7.8 collective-permute-done
  765.8 7.8 collective-permute-done
  781.3 7.8 collective-permute-done
  796.8 7.8 collective-permute-done
  812.3 7.8 collective-permute-done
  827.8 7.8 collective-permute-done
  843.3 7.8 collective-permute-done
  858.8 7.8 collective-permute-done
  874.3 7.8 collective-permute-done
  889.7 7.8 collective-permute-done
  920.7 7.8 collective-permute-done
  936.2 7.8 collective-permute-done
  951.7 7.8 collective-permute-done
  967.2 7.8 collective-permute-done
  982.7 7.8 collective-permute-done
  998.2 7.8 collective-permute-done
  1013.7 7.8 collective-permute-done
  1029.1 7.8 collective-permute-done
  1044.6 7.8 collective-permute-done
  1060.1 7.8 collective-permute-done
  1075.6 7.8 collective-permute-done
  1091.1 7.8 collective-permute-done
  1106.6 7.8 collective-permute-done
  1122.1 7.8 collective-permute-done
  1137.6 7.8 collective-permute-done
  (343 shorter events, 643.6 us)
Async XLA Ops:
  8.0 23.0 %all-gather.6.cloned.1.call-start = ((), (), s32[]{:S(2)}) async-start(), calls=%async_computation | async-start | bytes 6291456 | tf_op jit(solution)/shard_map/all_gather | solution.py:80
  12.0 154.6 %all-reduce.3.cloned.1.call-start = ((), (), s32[]{:S(2)}) async-start(), calls=%async_computation.4 | async-start | bytes 2097152
  16.8 152.9 %all-gather.8.cloned.1.call-start = ((), (), s32[]{:S(2)}) async-start(), calls=%async_computation.1 | async-start | bytes 12582912 | tf_op jit(solution)/shard_map/all_gather | solution.py:95
  90.2 110.7 %all-gather.12.cloned.1.call-start = ((), (), s32[]{:S(2)}) async-start(), calls=%async_computation.3 | async-start | bytes 6291456 | tf_op jit(solution)/shard_map/all_gather | solution.py:125
  185.1 46.3 %all-gather.10.cloned.1.call-start = ((), (), s32[]{:S(2)}) async-start(), calls=%async_computation.2 | async-start | bytes 6291456 | tf_op jit(solution)/shard_map/all_gather | solution.py:131
  237.3 9.7 collective-permute-start
  252.8 9.7 collective-permute-start
  268.3 9.7 collective-permute-start
  283.8 9.7 collective-permute-start
  299.3 9.7 collective-permute-start
  314.8 9.7 collective-permute-start
  330.2 9.7 collective-permute-start
  345.7 9.7 collective-permute-start
  361.2 9.7 collective-permute-start
  376.7 9.7 collective-permute-start
  392.2 9.7 collective-permute-start
  407.7 9.7 collective-permute-start
  423.2 9.7 collective-permute-start
  438.7 9.7 collective-permute-start
  454.2 9.7 collective-permute-start
  469.6 9.7 collective-permute-start
  485.1 9.7 collective-permute-start
  500.6 9.7 collective-permute-start
  516.1 9.7 collective-permute-start
  531.6 9.7 collective-permute-start
  547.1 9.7 collective-permute-start
  562.6 9.7 collective-permute-start
  578.1 9.7 collective-permute-start
  593.5 9.7 collective-permute-start
  609.0 9.7 collective-permute-start
  624.5 9.7 collective-permute-start
  640.0 9.7 collective-permute-start
  655.5 9.7 collective-permute-start
  671.0 9.7 collective-permute-start
  686.5 9.7 collective-permute-start
  702.0 9.7 collective-permute-start
  717.4 9.7 collective-permute-start
  732.9 9.7 collective-permute-start
  748.4 9.7 collective-permute-start
  763.9 9.7 collective-permute-start
  779.4 9.7 collective-permute-start
  794.9 9.7 collective-permute-start
  810.4 9.7 collective-permute-start
  825.9 9.7 collective-permute-start
  841.4 9.7 collective-permute-start
  856.8 9.7 collective-permute-start
  872.3 9.7 collective-permute-start
  887.8 9.7 collective-permute-start
  903.3 9.7 collective-permute-start
  918.8 9.7 collective-permute-start
  934.3 9.7 collective-permute-start
  949.8 9.7 collective-permute-start
  965.3 9.7 collective-permute-start
  980.7 9.7 collective-permute-start
  996.2 9.7 collective-permute-start
  1011.7 9.7 collective-permute-start
  1027.2 9.7 collective-permute-start
  1042.7 9.7 collective-permute-start
  1058.2 9.7 collective-permute-start
  1073.7 9.7 collective-permute-start
  1089.2 9.7 collective-permute-start
  1120.1 9.7 collective-permute-start
  1135.6 9.7 collective-permute-start
  1182.1 9.7 collective-permute-start
  (14 other events, 118.4 us)
Sparse Core Ops, SparseCore 0:
  12.2 18.8 all-gather.5
  90.4 23.9 all-gather.7
  185.2 15.6 all-gather.11
  211.8 17.6 all-gather.9
Sparse Core Ops, SparseCore 1:
  17.3 149.3 all-reduce.2
where the time goes:
time: 1270 us; the launch traced here: 1250 us
  waiting for transfers between devices  583 us (46%)
  matrix products  487 us (38%)
  starting transfers between devices  125 us (10%)
  local copies, waits for them, and re-layouts  19.4 us (2%)
  between operations  17.9 us (1%)
  other arithmetic  15 us (1%)
    ppermute x64, waiting for transfers between devices, shifted(): return lax.ppermute(block, axis, route)  493 us
    dot_general x63, matrix products, chain_turn(): outgoing = jnp.dot(composite, incoming, precision=finest_accuracy) + offset  362 us
    ppermute x64, starting transfers between devices, shifted(): return lax.ppermute(block, axis, route)  125 us
    unnamed x6, waiting for transfers between devices  71 us
    dot_general x3, matrix products, shards(): jnp.einsum('shk,skd->shd', section, jacobian, precision=finest_accuracy)  46.2 us
  transfers between devices with their start and end apart: 69, of which 67 were waited for; matrix products, arithmetic and copies ran while one was open for 8% of the time, Pallas kernels for 0%

commit v1 on v0

v1 whole, which is shorter than its diff:
```python
import functools

import jax
import jax.numpy as jnp
from jax import lax
from jax.experimental import pallas as pl
from jax.experimental.pallas import tpu as pltpu
from jax.sharding import PartitionSpec as P

F32 = jnp.float32
BF16 = jnp.bfloat16
MESH = pl.DeviceIdType.MESH
STEP = 0.25
LANES = 128
VMEM_BYTES = 67043328


def split(value):
    high = value.astype(BF16)
    return high, (value - high.astype(F32)).astype(BF16)


def dot3(left_high, left_low, right_high, right_low):
    dot = functools.partial(jnp.dot, preferred_element_type=F32)
    return dot(left_high, right_low) + dot(left_low, right_high) + dot(left_high, right_high)


def eye_rows(first_row, rows, width):
    row = lax.broadcasted_iota(jnp.int32, (rows, width), 0) + first_row
    return (row == lax.broadcasted_iota(jnp.int32, (rows, width), 1)).astype(F32)


def matvec(tile, vectors, out_blocks, groups):
    rows = [[] for _ in vectors]
    for block in range(out_blocks):
        totals = [None] * len(vectors)
        for group in range(groups):
            entries = tile(block, group)
            for index, vector in enumerate(vectors):
                term = entries * vector[group : group + 1, :]
                totals[index] = term if totals[index] is None else totals[index] + term
        for index, total in enumerate(totals):
            rows[index].append(jnp.sum(total.T, axis=0, keepdims=True))
    return [jnp.concatenate(found, axis=0) for found in rows]


def matvec_loop(tile, vectors, outs, out_blocks, groups):
    def block_turn(block, carry):
        for index, row in enumerate(matvec(lambda _, group: tile(block, group), vectors, 1, groups)):
            outs[index][pl.ds(block, 1), :] = row
        return carry

    lax.fori_loop(0, out_blocks, block_turn, 0)


def square(ref):
    def tile(block, group):
        start = block * LANES if isinstance(block, int) else pl.multiple_of(block * LANES, LANES)
        return ref[pl.ds(start, LANES), pl.ds(group * LANES, LANES)]

    return tile


def pair_tile(high, low):
    def tile(block, group):
        where = (pl.ds(pl.multiple_of(block * LANES, LANES), LANES), pl.ds(group * LANES, LANES))
        return high[where].astype(F32) + low[where].astype(F32)

    return tile


def kernel(
    dims,
    skew,
    gain_cross,
    gain_diag,
    smooth_cross,
    smooth_diag,
    init,
    obs_own,
    filtered,
    smoothed,
    skew_own,
    skew_far,
    a_high,
    a_low,
    b_high,
    b_low,
    w_high,
    w_low,
    g_full,
    m_full,
    g_high,
    g_low,
    tangent,
    p_high,
    p_low,
    composed,
    obs,
    share_wide,
    share,
    goal,
    gain_goal,
    offset,
    arrived,
    outgoing,
    state,
    work,
    result_own,
    result_far,
    later,
    local_sem,
    skew_sem,
    map_sem,
    obs_send,
    obs_recv,
    chain_send,
    chain_recv,
    last_send,
    far_recv,
    later_recv,
):
    turn = lax.axis_index("tm")
    core = lax.axis_index("row")
    turns = lax.axis_size("tm")
    width = gain_cross.shape[0]
    half = width // 2
    other = 1 - core
    size_x, size_z, size_y = dims

    def at(turn_id, core_id):
        return dict(device_id=(turn_id, core_id), device_id_type=MESH)

    def ring_peers(size, stride):
        here = lax.rem(turn // stride, size)
        return [turn + (lax.rem(here + shift, size) - here) * stride for shift in range(1, size)]

    rings = [(size_y, 1), (size_z, size_y), (size_x, size_y * size_z)]

    own_copy = pltpu.make_async_copy(
        skew.at[core], skew_own.at[pl.ds(core * half, half)], local_sem.at[0]
    )
    own_copy.start()
    gain_copy = pltpu.make_async_copy(gain_cross, g_full, local_sem.at[1])
    gain_copy.start()
    smooth_copy = pltpu.make_async_copy(smooth_cross, m_full, local_sem.at[2])
    smooth_copy.start()

    barrier = pltpu.get_barrier_semaphore()
    count = 1
    pl.semaphore_signal(barrier, inc=1, **at(turn, other))
    for size, stride in rings:
        for peer in ring_peers(size, stride):
            pl.semaphore_signal(barrier, inc=1, **at(peer, core))
            count += 1

    @pl.when(turn > 0)
    def _():
        for target in range(2):
            pl.semaphore_signal(barrier, inc=1, **at(turn - 1, target))

    @pl.when(turn < turns - 1)
    def _():
        for target in range(2):
            pl.semaphore_signal(barrier, inc=1, **at(turn + 1, target))

    slot = turn * 2 + core
    obs[pl.ds(slot, 1)] = obs_own[...]
    ends = jnp.where(turn > 0, 2, 0) + jnp.where(turn < turns - 1, 2, 0)
    pl.semaphore_wait(barrier, count + ends)

    skew_send = pltpu.make_async_remote_copy(
        src_ref=skew.at[other],
        dst_ref=skew_own.at[pl.ds(core * half, half)],
        send_sem=skew_sem.at[0],
        recv_sem=skew_sem.at[1],
        **at(turn, other),
    )
    skew_send.start()

    sent = []

    def obs_copy(first, rows, target, core_id, index):
        place = obs.at[pl.ds(first, rows)]
        copy = pltpu.make_async_remote_copy(
            src_ref=place,
            dst_ref=place,
            send_sem=obs_send.at[index],
            recv_sem=obs_recv.at[index],
            **at(target, core_id),
        )
        copy.start()
        sent.append(copy)
        return copy

    def obs_ring(number):
        size, stride = rings[number]
        rows = 2 * stride
        first = turn // stride * rows
        copies = []
        for index, peer in enumerate(ring_peers(size, stride)):
            copies.append(obs_copy(first, rows, peer, core, 1 + 3 * number + index))
        return copies

    core_copies = [obs_copy(slot, 1, turn, other, 0)]

    gain_copy.wait()

    def gain_turn(block, carry):
        rows = pl.ds(pl.multiple_of(block * LANES, LANES), LANES)
        value = g_full[rows, :] + eye_rows(block * LANES, LANES, width) * jnp.concatenate(
            [gain_diag[group : group + 1, :] for group in range(width // LANES)], axis=1
        )
        g_high[rows, :], g_low[rows, :] = split(value)
        return carry

    lax.fori_loop(0, width // LANES, gain_turn, 0)
    for copy in core_copies:
        copy.wait()
    ring_copies = obs_ring(0)
    own_copy.wait()
    skew_send.wait()

    def skew_turn(block, carry):
        rows = pl.ds(pl.multiple_of(block * LANES, LANES), LANES)
        value = STEP * (skew_own[rows, :].astype(F32) - skew_own[:, rows].astype(F32).T)
        a_high[rows, :], a_low[rows, :] = split(value)
        return carry

    lax.fori_loop(0, width // LANES, skew_turn, 0)
    for copy in ring_copies:
        copy.wait()
    ring_copies = obs_ring(1)

    strip = 256

    def square_turn(block, carry):
        rows = pl.ds(pl.multiple_of(block * strip, strip), strip)
        value = dot3(a_high[rows, :], a_low[rows, :], a_high[...], a_low[...])
        b_high[rows, :], b_low[rows, :] = split(value)
        a_value = a_high[rows, :].astype(F32) + a_low[rows, :].astype(F32)
        w_value = 0.5 * eye_rows(block * strip, strip, width) + a_value / 6.0 + value / 24.0
        w_high[rows, :], w_low[rows, :] = split(w_value)
        return carry

    lax.fori_loop(0, width // strip // 2, square_turn, 0)
    for copy in ring_copies:
        copy.wait()
    ring_copies = obs_ring(2)
    lax.fori_loop(width // strip // 2, width // strip, square_turn, 0)
    for copy in ring_copies:
        copy.wait()

    meta = obs[:, 1, :].T
    weighted = obs[:, 0, :]
    blocks = width // LANES
    block_ids = lax.broadcasted_iota(jnp.int32, (blocks, LANES), 0).astype(F32)
    for index in range(2):
        step = (turn * 2 + index).astype(F32)
        chosen = jnp.where((meta[1:2, :] == step) & (meta[2:3, :] == block_ids), 1.0, 0.0)
        weight = jnp.sum(chosen * meta[0:1, :], axis=1, keepdims=True)
        value = jnp.dot(chosen, weighted, precision=lax.Precision.HIGHEST, preferred_element_type=F32)
        share[index] = jnp.broadcast_to(weight / (weight + 1.0), (blocks, LANES))
        goal[index] = value / (weight + 1.0)
    for group in range(blocks):
        share_wide[:, group * LANES : (group + 1) * LANES] = share[core]

    def tangent_turn(block, carry):
        rows = pl.ds(pl.multiple_of(block * strip, strip), strip)
        value = dot3(b_high[rows, :], b_low[rows, :], w_high[...], w_low[...])
        a_value = a_high[rows, :].astype(F32) + a_low[rows, :].astype(F32)
        value = eye_rows(block * strip, strip, width) + a_value + value
        tangent[rows, :] = value
        return carry

    lax.fori_loop(0, width // strip, tangent_turn, 0)

    def shared_turn(block, carry):
        rows = pl.ds(pl.multiple_of(block * LANES, LANES), LANES)
        value = tangent[rows, :] * share_wide[pl.ds(block, 1), :]
        w_high[rows, :], w_low[rows, :] = split(value)
        return carry

    lax.fori_loop(0, blocks, shared_turn, 0)

    def map_copy(block, part):
        ref = (p_high, p_low)[part]
        place = ref.at[core, pl.ds(pl.multiple_of(block * strip, strip), strip)]
        return pltpu.make_async_remote_copy(
            src_ref=place,
            dst_ref=place,
            send_sem=map_sem.at[0, part],
            recv_sem=map_sem.at[1, part],
            **at(turn, other),
        )

    def map_turn(block, carry):
        rows = pl.ds(pl.multiple_of(block * strip, strip), strip)

        @pl.when(block > 0)
        def _():
            map_copy(block - 1, 0).start()
            map_copy(block - 1, 1).start()

        value = tangent[rows, :] - dot3(g_high[rows, :], g_low[rows, :], w_high[...], w_low[...])
        p_high[core, rows, :], p_low[core, rows, :] = split(value)
        return carry

    lax.fori_loop(0, width // strip, map_turn, 0)

    gain_tile = square(g_full)
    matvec_loop(gain_tile, [goal[0], goal[1]], [gain_goal.at[0], gain_goal.at[1]], blocks, blocks)
    for index in range(2):
        gain_goal[index] += gain_diag[...] * goal[index]
    map_copy(width // strip - 1, 0).start()
    map_copy(width // strip - 1, 1).start()
    for part in range(2):
        ref = (p_high, p_low)[part]
        whole = pltpu.make_async_remote_copy(
            src_ref=ref.at[core],
            dst_ref=ref.at[other],
            send_sem=map_sem.at[0, part],
            recv_sem=map_sem.at[1, part],
            **at(turn, other),
        )
        whole.wait_send()
        whole.wait_recv()
    columns = pl.ds(pl.multiple_of(core * half, half), half)

    def compose_turn(block, carry):
        rows = pl.ds(pl.multiple_of(block * strip, strip), strip)
        composed[rows, :] = dot3(
            p_high[1, rows, :], p_low[1, rows, :], p_high[0, :, columns], p_low[0, :, columns]
        )
        return carry

    lax.fori_loop(0, width // strip, compose_turn, 0)
    matvec_loop(pair_tile(p_high.at[1], p_low.at[1]), [gain_goal[0]], [offset], blocks, blocks)
    offset[...] = jnp.where(core == 0, offset[...] + gain_goal[1], 0.0)

    @pl.when(turn == 0)
    def _():
        state[...] = init[...]

    @pl.when(turn > 0)
    def _():
        pltpu.make_async_copy(arrived, arrived, chain_recv).wait()
        state[...] = arrived[0] + arrived[1]

    @pl.when(turn < turns - 1)
    def _():
        own_half = state[pl.ds(core * (blocks // 2), blocks // 2), :]
        outgoing[...] = matvec(square(composed), [own_half], blocks, blocks // 2)[0] + offset[...]
        for target in range(2):
            pltpu.make_async_remote_copy(
                src_ref=outgoing,
                dst_ref=arrived.at[core],
                send_sem=chain_send.at[target],
                recv_sem=chain_recv,
                **at(turn + 1, target),
            ).start()

    @pl.when(core == 1)
    def _():
        matvec_loop(pair_tile(p_high.at[0], p_low.at[0]), [state[...]], [work.at[0]], blocks, blocks)
        state[...] = work[0] + gain_goal[0]

    matvec_loop(square(tangent), [state[...]], [work.at[0]], blocks, blocks)
    missing = goal[core] - share[core] * work[0]
    matvec_loop(gain_tile, [missing], [work.at[1]], blocks, blocks)
    increment = work[1] + gain_diag[...] * missing
    result_own[0] = increment
    result_own[1] = work[0] + increment

    far_copy = pltpu.make_async_remote_copy(
        src_ref=result_own,
        dst_ref=result_far,
        send_sem=last_send.at[2],
        recv_sem=far_recv,
        **at(turn, other),
    )

    def later_copy(target):
        return pltpu.make_async_remote_copy(
            src_ref=result_own.at[0],
            dst_ref=later.at[core],
            send_sem=last_send.at[target],
            recv_sem=later_recv,
            **at(turn - 1, target),
        )

    @pl.when(turn > 0)
    def _():
        later_copy(0).start()
        later_copy(1).start()

    far_copy.start()

    @pl.when(turn == turns - 1)
    def _():
        later[...] = jnp.zeros_like(later)

    far_copy.wait()
    smooth_copy.wait()

    @pl.when(turn < turns - 1)
    def _():
        pltpu.make_async_copy(later, later, later_recv).wait()

    smooth_tile = square(m_full)
    matvec_loop(smooth_tile, [later[0], later[1]], [work.at[0], work.at[1]], blocks, blocks)
    second = jnp.where(core == 1, result_own[0], result_far[0])
    first_carried = second + work[0] + smooth_diag[...] * later[0]
    second_carried = later[0] + work[1] + smooth_diag[...] * later[1]
    work[0] = first_carried
    work[1] = second_carried
    part = pl.ds(core * (blocks // 2), blocks // 2)

    def half_tile(block, group):
        start = pl.multiple_of(core * half + block * LANES, LANES)
        return m_full[pl.ds(start, LANES), pl.ds(group * LANES, LANES)]

    matvec_loop(
        half_tile, [first_carried, second_carried], [smoothed.at[0], smoothed.at[1]], blocks // 2, blocks
    )
    diag_part = smooth_diag[part, :]
    for index in range(2):
        mean = jnp.where(core == index, result_own[1, part, :], result_far[1, part, :])
        filtered[index] = mean
        smoothed[index] = mean + smoothed[index] + diag_part * work[index, part, :]

    @pl.when(turn < turns - 1)
    def _():
        for target in range(2):
            pltpu.make_async_remote_copy(
                src_ref=outgoing,
                dst_ref=arrived.at[core],
                send_sem=chain_send.at[target],
                recv_sem=chain_recv,
                **at(turn + 1, target),
            ).wait_send()

    @pl.when(turn > 0)
    def _():
        later_copy(0).wait_send()
        later_copy(1).wait_send()


def shards(
    dims,
    init_mean,
    jac_skew,
    gain_diag,
    gain_cross,
    smooth_diag,
    smooth_cross,
    obs_values,
    obs_prec,
    obs_sensor,
    obs_block,
    sensor_step,
):
    width = jac_skew.shape[2]
    blocks = width // LANES
    hits = obs_sensor[:, None] == jnp.arange(sensor_step.shape[0], dtype=jnp.int32)[None, :]
    obs_step = jnp.sum(jnp.where(hits, sensor_step[None, :], 0), axis=1).astype(F32)
    lane = jnp.arange(LANES, dtype=jnp.int32)[None, :]
    meta = jnp.where(
        lane == 0,
        obs_prec[:, None],
        jnp.where(lane == 1, obs_step[:, None], obs_block[:, None].astype(F32)),
    )
    obs_own = jnp.stack([obs_prec[:, None] * obs_values, meta], axis=1)
    obs_total = lax.axis_size(("tm", "row"))
    vmem = pl.BlockSpec(memory_space=pltpu.VMEM)
    hbm = pl.BlockSpec(memory_space=pltpu.HBM)

    def wide(kind, lead=(), columns=width):
        return pltpu.VMEM(tuple(lead) + (width, columns), kind)

    def small(*lead):
        return pltpu.VMEM(tuple(lead) + (blocks, LANES), F32)

    dma = pltpu.SemaphoreType.DMA
    filtered, smoothed = pl.pallas_call(
        functools.partial(kernel, dims),
        out_shape=[jax.ShapeDtypeStruct((2, blocks // 2, LANES), F32)] * 2,
        in_specs=[hbm, hbm, vmem, hbm, vmem, vmem, vmem],
        out_specs=[vmem, vmem],
        scratch_shapes=[
            wide(BF16),
            pltpu.VMEM((8, LANES), F32),
            wide(BF16),
            wide(BF16),
            wide(BF16),
            wide(BF16),
            wide(BF16),
            wide(BF16),
            wide(F32),
            wide(F32),
            wide(BF16),
            wide(BF16),
            wide(F32),
            wide(BF16, (2,)),
            wide(BF16, (2,)),
            wide(F32, (), width // 2),
            pltpu.VMEM((obs_total, 2, LANES), F32),
            pltpu.VMEM((blocks, width), F32),
            small(2),
            small(2),
            small(2),
            small(),
            small(2),
            small(),
            small(),
            small(2),
            small(2),
            small(2),
            small(2),
            dma((3,)),
            dma((2,)),
            dma((2, 2)),
            dma((10,)),
            dma((10,)),
            dma((2,)),
            dma,
            dma((3,)),
            dma,
            dma,
        ],
        compiler_params=pltpu.CompilerParams(
            collective_id=0, has_side_effects=True, vmem_limit_bytes=VMEM_BYTES
        ),
    )(
        jac_skew,
        gain_cross,
        gain_diag.reshape(blocks, LANES),
        smooth_cross,
        smooth_diag.reshape(blocks, LANES),
        init_mean.reshape(blocks, LANES),
        obs_own,
    )
    return filtered.reshape(2, width // 2), smoothed.reshape(2, width // 2)


def solution(mesh):
    turns = mesh.shape["tm"]
    dims = {64: (4, 4, 4), 4: (1, 2, 2), 8: (2, 2, 2)}[turns]
    in_specs = (
        P(),
        P("tm", "row", None),
        P(),
        P(),
        P(),
        P(),
        P(("tm", "row"), None),
        P(("tm", "row")),
        P(("tm", "row")),
        P(("tm", "row")),
        P(),
    )
    out_specs = (P("tm", "row"), P("tm", "row"))
    return jax.shard_map(
        functools.partial(shards, dims),
        mesh=mesh,
        in_specs=in_specs,
        out_specs=out_specs,
        check_vma=False,
    )
```

time: 1270 us -> 253 us (0.20)
  the two profiles are of different devices: /device:TPU:2 before, /device:TPU:103 now
where the time goes in v1:
time: 253 us; the launch traced here: 249 us
  Pallas kernels  242 us (96%)
  between operations  3.15 us (1%)
  other arithmetic  2.55 us (1%)
    pallas_call x1, Pallas kernels, shards(): pl.pallas_call(functools.partial(kernel, dims), out_shape=[jax.ShapeDtype...  242 us

profile of v1, /device:TPU:103, one launch (start us, length us, event | category | flops | bytes accessed | tf_op | source)
XLA Modules:
  0.0 248.5 jit_solution(3598884894741399548)
XLA Ops:
  2.6 1.3 select_reduce_fusion
  4.5 0.7 multiply_bitcast_fusion
  5.1 0.6 pad_maximum_fusion.obs_own
  5.7 241.5 %shard_map.122 = (f32[2,4,128]{2,1,0:T(4,128)}, f32[2,4,128]{2,1,0:T(4,128)}) custom-call(bf16[2,512,1024]{2,1,0:T(8,128)(2,1)} %skew.1, f32[1024,1024]{1,0:T(8,128)} %gain_cross.1, f32[8,128]{1,0:T(8,128)} %bitcast.17, f32[1024,1024]{1,0:T(8,128)} %smooth_cross.1, f32[8,128]{1,0:T(8,128)} %bitcast.18, f32[8,128]{1,0:T(8,128)} %bitcast.19, ...), custom_call_target="tpu_custom_call" | custom-call | tf_op jit(solution)/shard_map/pallas_call | solution.py:485
  247.2 1.3 copy_bitcast_fusion
  (1 shorter events, 0.0 us)

commit v2 on v1

--- a/solution.py
+++ b/solution.py
@@ -13,6 +13,8 @@
 STEP = 0.25
 LANES = 128
 VMEM_BYTES = 67043328
+LEVELS = 32767.0
+dot = functools.partial(jnp.dot, preferred_element_type=F32)
 
 
 def split(value):
@@ -21,7 +23,6 @@
 
 
 def dot3(left_high, left_low, right_high, right_low):
-    dot = functools.partial(jnp.dot, preferred_element_type=F32)
     return dot(left_high, right_low) + dot(left_low, right_high) + dot(left_high, right_high)
 
 
@@ -77,11 +78,14 @@
     smooth_cross,
     smooth_diag,
     init,
-    obs_own,
+    obs_values,
+    obs_prec,
+    obs_sensor,
+    obs_block,
+    sensor_step,
     filtered,
     smoothed,
     skew_own,
-    skew_far,
     a_high,
     a_low,
     b_high,
@@ -96,12 +100,22 @@
     p_high,
     p_low,
     composed,
+    c_high,
+    c_low,
+    prefix,
+    coded_in,
+    coded_out,
+    scales_in,
+    scales_out,
     obs,
     share_wide,
     share,
     goal,
     gain_goal,
     offset,
+    offset_in,
+    partial_out,
+    partial_in,
     arrived,
     outgoing,
     state,
@@ -109,11 +123,17 @@
     result_own,
     result_far,
     later,
+    summed,
     local_sem,
     skew_sem,
     map_sem,
     obs_send,
     obs_recv,
+    whole_sem,
+    block_send,
+    block_recv,
+    offset_sem,
+    partial_sem,
     chain_send,
     chain_recv,
     last_send,
@@ -127,6 +147,17 @@
     half = width // 2
     other = 1 - core
     size_x, size_z, size_y = dims
+    blocks = width // LANES
+    parts = half // LANES
+    group = size_y
+    front = min(3, size_x * size_z - 1) * group
+    place = lax.rem(turn, group)
+    streams = turn >= front
+    source = jnp.where(streams, turn - place, turn) - 1
+    sends_one = turn < front - 1
+    sends_all = (turn == front - 1) | (streams & (place == group - 1) & (turn < turns - 1))
+    follows = streams & (place > 0)
+    leads = streams & (place == 0)
 
     def at(turn_id, core_id):
         return dict(device_id=(turn_id, core_id), device_id_type=MESH)
@@ -157,7 +188,7 @@
     @pl.when(turn > 0)
     def _():
         for target in range(2):
-            pl.semaphore_signal(barrier, inc=1, **at(turn - 1, target))
+            pl.semaphore_signal(barrier, inc=1, **at(source, target))
 
     @pl.when(turn < turns - 1)
     def _():
@@ -165,8 +196,18 @@
             pl.semaphore_signal(barrier, inc=1, **at(turn + 1, target))
 
     slot = turn * 2 + core
-    obs[pl.ds(slot, 1)] = obs_own[...]
-    ends = jnp.where(turn > 0, 2, 0) + jnp.where(turn < turns - 1, 2, 0)
+    sensor_ids = lax.broadcasted_iota(jnp.int32, sensor_step.shape, 0) * LANES
+    sensor_ids += lax.broadcasted_iota(jnp.int32, sensor_step.shape, 1)
+    found = jnp.where(sensor_ids == obs_sensor[0], sensor_step[...], 0).astype(F32)
+    found = jnp.sum(jnp.sum(found, axis=0, keepdims=True), axis=1, keepdims=True)
+    lane = lax.broadcasted_iota(jnp.int32, (1, LANES), 1)
+    meta_row = jnp.where(
+        lane == 0, obs_prec[0], jnp.where(lane == 1, found, obs_block[0].astype(F32))
+    )
+    obs[slot, 0:1, :] = obs_prec[0] * obs_values[...]
+    obs[slot, 1:2, :] = meta_row
+    ends = jnp.where(turn > 0, 2, 0) + jnp.where(sends_one, 2, 0)
+    ends += jnp.where(sends_all, 2 * group, 0)
     pl.semaphore_wait(barrier, count + ends)
 
     skew_send = pltpu.make_async_remote_copy(
@@ -181,10 +222,10 @@
     sent = []
 
     def obs_copy(first, rows, target, core_id, index):
-        place = obs.at[pl.ds(first, rows)]
+        rows_ref = obs.at[pl.ds(first, rows)]
         copy = pltpu.make_async_remote_copy(
-            src_ref=place,
-            dst_ref=place,
+            src_ref=rows_ref,
+            dst_ref=rows_ref,
             send_sem=obs_send.at[index],
             recv_sem=obs_recv.at[index],
             **at(target, core_id),
@@ -253,7 +294,6 @@
 
     meta = obs[:, 1, :].T
     weighted = obs[:, 0, :]
-    blocks = width // LANES
     block_ids = lax.broadcasted_iota(jnp.int32, (blocks, LANES), 0).astype(F32)
     for index in range(2):
         step = (turn * 2 + index).astype(F32)
@@ -262,8 +302,8 @@
         value = jnp.dot(chosen, weighted, precision=lax.Precision.HIGHEST, preferred_element_type=F32)
         share[index] = jnp.broadcast_to(weight / (weight + 1.0), (blocks, LANES))
         goal[index] = value / (weight + 1.0)
-    for group in range(blocks):
-        share_wide[:, group * LANES : (group + 1) * LANES] = share[core]
+    for column in range(blocks):
+        share_wide[:, column * LANES : (column + 1) * LANES] = share[core]
 
     def tangent_turn(block, carry):
         rows = pl.ds(pl.multiple_of(block * strip, strip), strip)
@@ -285,10 +325,10 @@
 
     def map_copy(block, part):
         ref = (p_high, p_low)[part]
-        place = ref.at[core, pl.ds(pl.multiple_of(block * strip, strip), strip)]
+        strip_ref = ref.at[core, pl.ds(pl.multiple_of(block * strip, strip), strip)]
         return pltpu.make_async_remote_copy(
-            src_ref=place,
-            dst_ref=place,
+            src_ref=strip_ref,
+            dst_ref=strip_ref,
             send_sem=map_sem.at[0, part],
             recv_sem=map_sem.at[1, part],
             **at(turn, other),
@@ -325,18 +365,127 @@
         )
         whole.wait_send()
         whole.wait_recv()
-    columns = pl.ds(pl.multiple_of(core * half, half), half)
+
+    def eye_block(block):
+        row = lax.broadcasted_iota(jnp.int32, (width, LANES), 0) - (core * half + block * LANES)
+        return row == lax.broadcasted_iota(jnp.int32, (width, LANES), 1)
+
+    def block_copies(block):
+        return [
+            pltpu.make_async_remote_copy(
+                src_ref=out_ref.at[block],
+                dst_ref=in_ref.at[block],
+                send_sem=block_send.at[block, index],
+                recv_sem=block_recv.at[block, index],
+                **at(turn + 1, core),
+            )
+            for index, (out_ref, in_ref) in enumerate(
+                ((coded_out, coded_in), (scales_out, scales_in))
+            )
+        ]
+
+    def send_block(value, block):
+        diagonal = eye_block(block)
+        rest = jnp.where(diagonal, 0.0, value)
+        largest = jnp.max(jnp.abs(rest), axis=0, keepdims=True)
+        factor = jnp.where(largest > 1e-30, LEVELS / jnp.maximum(largest, 1e-30), 0.0)
+        coded_out[block] = jnp.round(rest * factor).astype(jnp.int32).astype(jnp.int16)
+        scales_out[block, 0:1, :] = largest * (1.0 / LEVELS)
+        scales_out[block, 1:2, :] = jnp.sum(value - rest, axis=0, keepdims=True)
+        for copy in block_copies(block):
+            copy.start()
+
+    def product(left_high, left_low, right_high, right_low):
+        both = dot(left_high, jnp.concatenate([right_high, right_low], axis=1))
+        return (both[:, LANES:] + dot(left_low, right_high)) + both[:, :LANES]
+
+    def lane_block(start):
+        return pl.ds(pl.multiple_of(start, LANES), LANES)
 
     def compose_turn(block, carry):
-        rows = pl.ds(pl.multiple_of(block * strip, strip), strip)
-        composed[rows, :] = dot3(
-            p_high[1, rows, :], p_low[1, rows, :], p_high[0, :, columns], p_low[0, :, columns]
+        columns = lane_block(core * half + block * LANES)
+        own = lane_block(block * LANES)
+        value = product(p_high[1], p_low[1], p_high[0, :, columns], p_low[0, :, columns])
+        composed[:, own] = value
+        c_high[core, :, own], c_low[core, :, own] = split(value)
+
+        @pl.when(leads)
+        def _():
+            send_block(value, block)
+
+        return carry
+
+    lax.fori_loop(0, parts, compose_turn, 0)
+    whole_copies = [
+        pltpu.make_async_remote_copy(
+            src_ref=ref.at[core],
+            dst_ref=ref.at[core],
+            send_sem=whole_sem.at[0, index],
+            recv_sem=whole_sem.at[1, index],
+            **at(turn, other),
         )
-        return carry
-
-    lax.fori_loop(0, width // strip, compose_turn, 0)
+        for index, ref in enumerate((c_high, c_low))
+    ]
+
+    @pl.when(follows)
+    def _():
+        for copy in whole_copies:
+            copy.start()
+
     matvec_loop(pair_tile(p_high.at[1], p_low.at[1]), [gain_goal[0]], [offset], blocks, blocks)
-    offset[...] = jnp.where(core == 0, offset[...] + gain_goal[1], 0.0)
+    offset[...] += gain_goal[1]
+    offset_copy = pltpu.make_async_remote_copy(
+        src_ref=offset,
+        dst_ref=offset_in,
+        send_sem=offset_sem.at[0],
+        recv_sem=offset_sem.at[1],
+        **at(turn + 1, core),
+    )
+
+    @pl.when(leads)
+    def _():
+        offset_copy.start()
+
+    @pl.when(follows)
+    def _():
+        for copy in whole_copies:
+            copy.wait()
+
+        def stream_turn(block, carry):
+            own = lane_block(block * LANES)
+            for copy in block_copies(block):
+                copy.wait_recv()
+            value = coded_in[block].astype(jnp.int32).astype(F32) * scales_in[block, 0:1, :]
+            value += jnp.where(eye_block(block), scales_in[block, 1:2, :], 0.0)
+            prefix[:, own] = value
+            high, low = split(value)
+            value = product(c_high[0], c_low[0], high[:half], low[:half])
+            value += product(c_high[1], c_low[1], high[half:], low[half:])
+
+            @pl.when(place < group - 1)
+            def _():
+                send_block(value, block)
+
+            @pl.when(place == group - 1)
+            def _():
+                composed[:, own] = value
+
+            return carry
+
+        lax.fori_loop(0, parts, stream_turn, 0)
+        offset_copy.wait_recv()
+
+        def whole_tile(block, column):
+            rows = pl.ds(pl.multiple_of(block * LANES, LANES), LANES)
+            where = (column // parts, rows, pl.ds(column % parts * LANES, LANES))
+            return c_high[where].astype(F32) + c_low[where].astype(F32)
+
+        matvec_loop(whole_tile, [offset_in[...]], [work.at[0]], blocks, blocks)
+        offset[...] += work[0]
+
+        @pl.when(place < group - 1)
+        def _():
+            offset_copy.start()
 
     @pl.when(turn == 0)
     def _():
@@ -347,18 +496,52 @@
         pltpu.make_async_copy(arrived, arrived, chain_recv).wait()
         state[...] = arrived[0] + arrived[1]
 
-    @pl.when(turn < turns - 1)
-    def _():
-        own_half = state[pl.ds(core * (blocks // 2), blocks // 2), :]
-        outgoing[...] = matvec(square(composed), [own_half], blocks, blocks // 2)[0] + offset[...]
-        for target in range(2):
+    own_half = pl.ds(core * parts, parts)
+
+    def chain_copies(count):
+        order = [count - 1] + list(range(count - 1))
+        return [
             pltpu.make_async_remote_copy(
                 src_ref=outgoing,
                 dst_ref=arrived.at[core],
-                send_sem=chain_send.at[target],
+                send_sem=chain_send.at[2 * step + target],
                 recv_sem=chain_recv,
-                **at(turn + 1, target),
-            ).start()
+                **at(turn + 1 + step, target),
+            )
+            for step in order
+            for target in range(2)
+        ]
+
+    @pl.when(sends_one | sends_all)
+    def _():
+        moved = matvec(square(composed), [state[own_half, :]], blocks, parts)[0]
+        outgoing[...] = moved + jnp.where(core == 0, offset[...], 0.0)
+
+    @pl.when(sends_one)
+    def _():
+        for copy in chain_copies(1):
+            copy.start()
+
+    @pl.when(sends_all)
+    def _():
+        for copy in chain_copies(group):
+            copy.start()
+
+    partial_copy = pltpu.make_async_remote_copy(
+        src_ref=partial_out,
+        dst_ref=partial_in,
+        send_sem=partial_sem.at[0],
+        recv_sem=partial_sem.at[1],
+        **at(turn, other),
+    )
+
+    @pl.when(follows)
+    def _():
+        moved = matvec(square(prefix), [state[own_half, :]], blocks, parts)[0]
+        partial_out[...] = moved + jnp.where(core == 0, offset_in[...], 0.0)
+        partial_copy.start()
+        partial_copy.wait()
+        state[...] = partial_out[...] + partial_in[...]
 
     @pl.when(core == 1)
     def _():
@@ -421,24 +604,33 @@
         return m_full[pl.ds(start, LANES), pl.ds(group * LANES, LANES)]
 
     matvec_loop(
-        half_tile, [first_carried, second_carried], [smoothed.at[0], smoothed.at[1]], blocks // 2, blocks
+        half_tile, [first_carried, second_carried], [summed.at[0], summed.at[1]], blocks // 2, blocks
     )
     diag_part = smooth_diag[part, :]
     for index in range(2):
         mean = jnp.where(core == index, result_own[1, part, :], result_far[1, part, :])
-        filtered[index] = mean
-        smoothed[index] = mean + smoothed[index] + diag_part * work[index, part, :]
-
-    @pl.when(turn < turns - 1)
-    def _():
-        for target in range(2):
-            pltpu.make_async_remote_copy(
-                src_ref=outgoing,
-                dst_ref=arrived.at[core],
-                send_sem=chain_send.at[target],
-                recv_sem=chain_recv,
-                **at(turn + 1, target),
-            ).wait_send()
+        late = mean + summed[index] + diag_part * work[index, part, :]
+        for column in range(blocks // 2):
+            where = (pl.ds(index, 1), pl.ds(column * LANES, LANES))
+            filtered[where] = mean[column : column + 1, :]
+            smoothed[where] = late[column : column + 1, :]
+
+    @pl.when(leads | (follows & (place < group - 1)))
+    def _():
+        for block in range(parts):
+            for copy in block_copies(block):
+                copy.wait_send()
+        offset_copy.wait_send()
+
+    @pl.when(sends_one)
+    def _():
+        for copy in chain_copies(1):
+            copy.wait_send()
+
+    @pl.when(sends_all)
+    def _():
+        for copy in chain_copies(group):
+            copy.wait_send()
 
     @pl.when(turn > 0)
     def _():
@@ -462,18 +654,12 @@
 ):
     width = jac_skew.shape[2]
     blocks = width // LANES
-    hits = obs_sensor[:, None] == jnp.arange(sensor_step.shape[0], dtype=jnp.int32)[None, :]
-    obs_step = jnp.sum(jnp.where(hits, sensor_step[None, :], 0), axis=1).astype(F32)
-    lane = jnp.arange(LANES, dtype=jnp.int32)[None, :]
-    meta = jnp.where(
-        lane == 0,
-        obs_prec[:, None],
-        jnp.where(lane == 1, obs_step[:, None], obs_block[:, None].astype(F32)),
-    )
-    obs_own = jnp.stack([obs_prec[:, None] * obs_values, meta], axis=1)
     obs_total = lax.axis_size(("tm", "row"))
     vmem = pl.BlockSpec(memory_space=pltpu.VMEM)
+    smem = pl.BlockSpec(memory_space=pltpu.SMEM)
     hbm = pl.BlockSpec(memory_space=pltpu.HBM)
+    parts = blocks // 2
+    group = dims[2]
 
     def wide(kind, lead=(), columns=width):
         return pltpu.VMEM(tuple(lead) + (width, columns), kind)
@@ -484,12 +670,11 @@
     dma = pltpu.SemaphoreType.DMA
     filtered, smoothed = pl.pallas_call(
         functools.partial(kernel, dims),
-        out_shape=[jax.ShapeDtypeStruct((2, blocks // 2, LANES), F32)] * 2,
-        in_specs=[hbm, hbm, vmem, hbm, vmem, vmem, vmem],
+        out_shape=[jax.ShapeDtypeStruct((2, width // 2), F32)] * 2,
+        in_specs=[hbm, hbm, vmem, hbm, vmem, vmem, vmem, smem, smem, smem, vmem],
         out_specs=[vmem, vmem],
         scratch_shapes=[
             wide(BF16),
-            pltpu.VMEM((8, LANES), F32),
             wide(BF16),
             wide(BF16),
             wide(BF16),
@@ -504,11 +689,21 @@
             wide(BF16, (2,)),
             wide(BF16, (2,)),
             wide(F32, (), width // 2),
+            wide(BF16, (2,), width // 2),
+            wide(BF16, (2,), width // 2),
+            wide(F32, (), width // 2),
+            wide(jnp.int16, (parts,), LANES),
+            wide(jnp.int16, (parts,), LANES),
+            pltpu.VMEM((parts, 2, LANES), F32),
+            pltpu.VMEM((parts, 2, LANES), F32),
             pltpu.VMEM((obs_total, 2, LANES), F32),
             pltpu.VMEM((blocks, width), F32),
             small(2),
             small(2),
             small(2),
+            small(),
+            small(),
+            small(),
             small(),
             small(2),
             small(),
@@ -517,12 +712,18 @@
             small(2),
             small(2),
             small(2),
+            pltpu.VMEM((2, parts, LANES), F32),
             dma((3,)),
             dma((2,)),
             dma((2, 2)),
             dma((10,)),
             dma((10,)),
+            dma((2, 2)),
+            dma((parts, 2)),
+            dma((parts, 2)),
             dma((2,)),
+            dma((2,)),
+            dma((2 * group,)),
             dma,
             dma((3,)),
             dma,
@@ -538,9 +739,13 @@
         smooth_cross,
         smooth_diag.reshape(blocks, LANES),
         init_mean.reshape(blocks, LANES),
-        obs_own,
-    )
-    return filtered.reshape(2, width // 2), smoothed.reshape(2, width // 2)
+        obs_values,
+        obs_prec,
+        obs_sensor,
+        obs_block,
+        sensor_step.reshape(-1, LANES),
+    )
+    return filtered, smoothed
 
 
 def solution(mesh):

time: 253 us -> 136 us (0.54); the launches traced: 249 us -> 136 us
  Pallas kernels: 242 us -> 131 us
  other arithmetic: 2.55 us -> 0 us
    pallas_call x1, Pallas kernels: 242 us -> 131 us  [shards(): pl.pallas_call(functools.partial(kernel, dims), out_shape=[jax.ShapeDtype...]
where the time goes in v2:
time: 136 us
  Pallas kernels  131 us (96%)
  between operations  2.58 us (2%)
  local copies, waits for them, and re-layouts  2.53 us (2%)
    pallas_call x1, Pallas kernels, shards(): pl.pallas_call(functools.partial(kernel, dims), out_shape=[jax.ShapeDtype...  131 us

profile of v2, /device:TPU:103, one launch (start us, length us, event | category | flops | bytes accessed | tf_op | source)
XLA Modules:
  0.0 136.0 jit_solution(6452880893312660287)
XLA Ops:
  2.6 130.9 %shard_map.122 = (f32[2,512]{1,0:T(2,128)}, f32[2,512]{1,0:T(2,128)}) custom-call(bf16[2,512,1024]{2,1,0:T(8,128)(2,1)} %skew.1, f32[1024,1024]{1,0:T(8,128)} %gain_cross.1, f32[8,128]{1,0:T(8,128)} %bitcast.4, f32[1024,1024]{1,0:T(8,128)} %smooth_cross.1, f32[8,128]{1,0:T(8,128)} %bitcast.5, f32[8,128]{1,0:T(8,128)} %bitcast.6, f32[1,128]{1,0:T(1,128)} %obs_values.1, ...), custom_call_target="tpu_custom_call" | custom-call | tf_op jit(solution)/shard_map/pallas_call | solution.py:671
  133.5 1.3 copy.18
  134.7 1.3 copy.19

commit v3 on v2

--- a/solution.py
+++ b/solution.py
@@ -14,6 +14,8 @@
 LANES = 128
 VMEM_BYTES = 67043328
 LEVELS = 32767.0
+CHUNK = 64
+UNROLL = 4
 dot = functools.partial(jnp.dot, preferred_element_type=F32)
 
 
@@ -46,12 +48,15 @@
 
 
 def matvec_loop(tile, vectors, outs, out_blocks, groups):
-    def block_turn(block, carry):
-        for index, row in enumerate(matvec(lambda _, group: tile(block, group), vectors, 1, groups)):
-            outs[index][pl.ds(block, 1), :] = row
+    def block_turn(turn, carry):
+        first = turn * UNROLL
+        found = matvec(lambda block, group: tile(first + block, group), vectors, UNROLL, groups)
+        for index, rows in enumerate(found):
+            for block in range(UNROLL):
+                outs[index][pl.ds(first + block, 1), :] = rows[block : block + 1]
         return carry
 
-    lax.fori_loop(0, out_blocks, block_turn, 0)
+    lax.fori_loop(0, out_blocks // UNROLL, block_turn, 0)
 
 
 def square(ref):
@@ -83,8 +88,7 @@
     obs_sensor,
     obs_block,
     sensor_step,
-    filtered,
-    smoothed,
+    result,
     skew_own,
     a_high,
     a_low,
@@ -107,6 +111,8 @@
     coded_out,
     scales_in,
     scales_out,
+    turned_in,
+    turned_out,
     obs,
     share_wide,
     share,
@@ -149,6 +155,7 @@
     size_x, size_z, size_y = dims
     blocks = width // LANES
     parts = half // LANES
+    chunks = half // CHUNK
     group = size_y
     front = min(3, size_x * size_z - 1) * group
     place = lax.rem(turn, group)
@@ -269,9 +276,6 @@
         return carry
 
     lax.fori_loop(0, width // LANES, skew_turn, 0)
-    for copy in ring_copies:
-        copy.wait()
-    ring_copies = obs_ring(1)
 
     strip = 256
 
@@ -287,8 +291,21 @@
     lax.fori_loop(0, width // strip // 2, square_turn, 0)
     for copy in ring_copies:
         copy.wait()
+    ring_copies = obs_ring(1)
+    lax.fori_loop(width // strip // 2, width // strip, square_turn, 0)
+    for copy in ring_copies:
+        copy.wait()
     ring_copies = obs_ring(2)
-    lax.fori_loop(width // strip // 2, width // strip, square_turn, 0)
+
+    def tangent_turn(block, carry):
+        rows = pl.ds(pl.multiple_of(block * strip, strip), strip)
+        value = dot3(b_high[rows, :], b_low[rows, :], w_high[...], w_low[...])
+        a_value = a_high[rows, :].astype(F32) + a_low[rows, :].astype(F32)
+        value = eye_rows(block * strip, strip, width) + a_value + value
+        tangent[rows, :] = value
+        return carry
+
+    lax.fori_loop(0, width // strip, tangent_turn, 0)
     for copy in ring_copies:
         copy.wait()
 
@@ -304,16 +321,6 @@
         goal[index] = value / (weight + 1.0)
     for column in range(blocks):
         share_wide[:, column * LANES : (column + 1) * LANES] = share[core]
-
-    def tangent_turn(block, carry):
-        rows = pl.ds(pl.multiple_of(block * strip, strip), strip)
-        value = dot3(b_high[rows, :], b_low[rows, :], w_high[...], w_low[...])
-        a_value = a_high[rows, :].astype(F32) + a_low[rows, :].astype(F32)
-        value = eye_rows(block * strip, strip, width) + a_value + value
-        tangent[rows, :] = value
-        return carry
-
-    lax.fori_loop(0, width // strip, tangent_turn, 0)
 
     def shared_turn(block, carry):
         rows = pl.ds(pl.multiple_of(block * LANES, LANES), LANES)
@@ -367,8 +374,8 @@
         whole.wait_recv()
 
     def eye_block(block):
-        row = lax.broadcasted_iota(jnp.int32, (width, LANES), 0) - (core * half + block * LANES)
-        return row == lax.broadcasted_iota(jnp.int32, (width, LANES), 1)
+        row = lax.broadcasted_iota(jnp.int32, (CHUNK, width), 0) + core * half + block * CHUNK
+        return row == lax.broadcasted_iota(jnp.int32, (CHUNK, width), 1)
 
     def block_copies(block):
         return [
@@ -404,34 +411,20 @@
 
     def compose_turn(block, carry):
         columns = lane_block(core * half + block * LANES)
-        own = lane_block(block * LANES)
         value = product(p_high[1], p_low[1], p_high[0, :, columns], p_low[0, :, columns])
-        composed[:, own] = value
-        c_high[core, :, own], c_low[core, :, own] = split(value)
+        composed[:, lane_block(block * LANES)] = value
+        turned = value.T
+        c_high[columns, :], c_low[columns, :] = split(turned)
 
         @pl.when(leads)
         def _():
-            send_block(value, block)
+            for index in range(LANES // CHUNK):
+                chunk = turned[index * CHUNK : (index + 1) * CHUNK]
+                send_block(chunk, block * (LANES // CHUNK) + index)
 
         return carry
 
-    lax.fori_loop(0, parts, compose_turn, 0)
-    whole_copies = [
-        pltpu.make_async_remote_copy(
-            src_ref=ref.at[core],
-            dst_ref=ref.at[core],
-            send_sem=whole_sem.at[0, index],
-            recv_sem=whole_sem.at[1, index],
-            **at(turn, other),
-        )
-        for index, ref in enumerate((c_high, c_low))
-    ]
-
-    @pl.when(follows)
-    def _():
-        for copy in whole_copies:
-            copy.start()
-
+    lax.fori_loop(0, 1, compose_turn, 0)
     matvec_loop(pair_tile(p_high.at[1], p_low.at[1]), [gain_goal[0]], [offset], blocks, blocks)
     offset[...] += gain_goal[1]
     offset_copy = pltpu.make_async_remote_copy(
@@ -446,46 +439,74 @@
     def _():
         offset_copy.start()
 
+    lax.fori_loop(1, parts, compose_turn, 0)
+    own_rows = pl.ds(pl.multiple_of(core * half, half), half)
+    whole_copies = [
+        pltpu.make_async_remote_copy(
+            src_ref=ref.at[own_rows],
+            dst_ref=ref.at[own_rows],
+            send_sem=whole_sem.at[0, index],
+            recv_sem=whole_sem.at[1, index],
+            **at(turn, other),
+        )
+        for index, ref in enumerate((c_high, c_low))
+    ]
+
+    @pl.when(follows)
+    def _():
+        for copy in whole_copies:
+            copy.start()
+
     @pl.when(follows)
     def _():
         for copy in whole_copies:
             copy.wait()
 
-        def stream_turn(block, carry):
-            own = lane_block(block * LANES)
-            for copy in block_copies(block):
-                copy.wait_recv()
-            value = coded_in[block].astype(jnp.int32).astype(F32) * scales_in[block, 0:1, :]
-            value += jnp.where(eye_block(block), scales_in[block, 1:2, :], 0.0)
-            prefix[:, own] = value
-            high, low = split(value)
-            value = product(c_high[0], c_low[0], high[:half], low[:half])
-            value += product(c_high[1], c_low[1], high[half:], low[half:])
-
-            @pl.when(place < group - 1)
-            def _():
-                send_block(value, block)
-
-            @pl.when(place == group - 1)
-            def _():
-                composed[:, own] = value
-
-            return carry
-
-        lax.fori_loop(0, parts, stream_turn, 0)
         offset_copy.wait_recv()
-
-        def whole_tile(block, column):
-            rows = pl.ds(pl.multiple_of(block * LANES, LANES), LANES)
-            where = (column // parts, rows, pl.ds(column % parts * LANES, LANES))
-            return c_high[where].astype(F32) + c_low[where].astype(F32)
-
-        matvec_loop(whole_tile, [offset_in[...]], [work.at[0]], blocks, blocks)
-        offset[...] += work[0]
+        row = jnp.concatenate([offset_in[block : block + 1, :] for block in range(blocks)], axis=1)
+        high = row.astype(BF16).astype(F32)
+        empty = jnp.zeros((6, width), F32)
+        left = jnp.concatenate([high, row - high, empty], axis=0).astype(BF16)
+        both = dot(left, c_high[...])
+        row = both[0:1] + (both[1:2] + dot(left, c_low[...])[0:1])
+        for block in range(blocks):
+            offset[block : block + 1, :] += row[:, block * LANES : (block + 1) * LANES]
 
         @pl.when(place < group - 1)
         def _():
             offset_copy.start()
+
+        def stream_turn(lane_index, carry):
+            columns = lane_block(lane_index * LANES)
+            for index in range(LANES // CHUNK):
+                block = lane_index * (LANES // CHUNK) + index
+                for copy in block_copies(block):
+                    copy.wait_recv()
+                value = coded_in[block].astype(jnp.int32).astype(F32) * scales_in[block, 0:1, :]
+                value += jnp.where(eye_block(block), scales_in[block, 1:2, :], 0.0)
+                rows = pl.ds(index * CHUNK, CHUNK)
+                turned_in[rows, :] = value
+                high, low = split(value)
+                both = dot(jnp.concatenate([high, low], axis=0), c_high[...])
+                value = both[:CHUNK] + (both[CHUNK:] + dot(high, c_low[...]))
+
+                @pl.when(place < group - 1)
+                def _():
+                    send_block(value, block)
+
+                @pl.when(place == group - 1)
+                def _():
+                    turned_out[rows, :] = value
+
+            prefix[:, columns] = turned_in[...].T
+
+            @pl.when(place == group - 1)
+            def _():
+                composed[:, columns] = turned_out[...].T
+
+            return carry
+
+        lax.fori_loop(0, parts, stream_turn, 0)
 
     @pl.when(turn == 0)
     def _():
@@ -611,13 +632,13 @@
         mean = jnp.where(core == index, result_own[1, part, :], result_far[1, part, :])
         late = mean + summed[index] + diag_part * work[index, part, :]
         for column in range(blocks // 2):
-            where = (pl.ds(index, 1), pl.ds(column * LANES, LANES))
-            filtered[where] = mean[column : column + 1, :]
-            smoothed[where] = late[column : column + 1, :]
+            columns = pl.ds(column * LANES, LANES)
+            result[index : index + 1, columns] = mean[column : column + 1, :]
+            result[index + 2 : index + 3, columns] = late[column : column + 1, :]
 
     @pl.when(leads | (follows & (place < group - 1)))
     def _():
-        for block in range(parts):
+        for block in range(chunks):
             for copy in block_copies(block):
                 copy.wait_send()
         offset_copy.wait_send()
@@ -658,7 +679,7 @@
     vmem = pl.BlockSpec(memory_space=pltpu.VMEM)
     smem = pl.BlockSpec(memory_space=pltpu.SMEM)
     hbm = pl.BlockSpec(memory_space=pltpu.HBM)
-    parts = blocks // 2
+    chunks = width // 2 // CHUNK
     group = dims[2]
 
     def wide(kind, lead=(), columns=width):
@@ -668,11 +689,11 @@
         return pltpu.VMEM(tuple(lead) + (blocks, LANES), F32)
 
     dma = pltpu.SemaphoreType.DMA
-    filtered, smoothed = pl.pallas_call(
+    result = pl.pallas_call(
         functools.partial(kernel, dims),
-        out_shape=[jax.ShapeDtypeStruct((2, width // 2), F32)] * 2,
+        out_shape=jax.ShapeDtypeStruct((4, width // 2), F32),
         in_specs=[hbm, hbm, vmem, hbm, vmem, vmem, vmem, smem, smem, smem, vmem],
-        out_specs=[vmem, vmem],
+        out_specs=vmem,
         scratch_shapes=[
             wide(BF16),
             wide(BF16),
@@ -689,13 +710,15 @@
             wide(BF16, (2,)),
             wide(BF16, (2,)),
             wide(F32, (), width // 2),
-            wide(BF16, (2,), width // 2),
-            wide(BF16, (2,), width // 2),
+            wide(BF16),
+            wide(BF16),
             wide(F32, (), width // 2),
-            wide(jnp.int16, (parts,), LANES),
-            wide(jnp.int16, (parts,), LANES),
-            pltpu.VMEM((parts, 2, LANES), F32),
-            pltpu.VMEM((parts, 2, LANES), F32),
+            pltpu.VMEM((chunks, CHUNK, width), jnp.int16),
+            pltpu.VMEM((chunks, CHUNK, width), jnp.int16),
+            pltpu.VMEM((chunks, 2, width), F32),
+            pltpu.VMEM((chunks, 2, width), F32),
+            pltpu.VMEM((LANES, width), F32),
+            pltpu.VMEM((LANES, width), F32),
             pltpu.VMEM((obs_total, 2, LANES), F32),
             pltpu.VMEM((blocks, width), F32),
             small(2),
@@ -712,15 +735,15 @@
             small(2),
             small(2),
             small(2),
-            pltpu.VMEM((2, parts, LANES), F32),
+            pltpu.VMEM((2, blocks // 2, LANES), F32),
             dma((3,)),
             dma((2,)),
             dma((2, 2)),
             dma((10,)),
             dma((10,)),
             dma((2, 2)),
-            dma((parts, 2)),
-            dma((parts, 2)),
+            dma((chunks, 2)),
+            dma((chunks, 2)),
             dma((2,)),
             dma((2,)),
             dma((2 * group,)),
@@ -745,7 +768,7 @@
         obs_block,
         sensor_step.reshape(-1, LANES),
     )
-    return filtered, smoothed
+    return result[:2], result[2:]
 
 
 def solution(mesh):

time: 136 us -> 129 us (0.949)
  Pallas kernels: 131 us -> 125 us
    pallas_call x1, Pallas kernels: 131 us -> 125 us  [shards(): pl.pallas_call(functools.partial(kernel, dims), out_shape=jax.ShapeDtypeS...]
    unnamed x2 -> x0, local copies, waits for them, and re-layouts: 2.53 us -> none
    slice x0 -> x1, local copies, waits for them, and re-layouts: none -> 1.37 us  [shards(): return (result[:2], result[2:])]
where the time goes in v3:
time: 129 us
  Pallas kernels  125 us (97%)
  between operations  2.58 us (2%)
  local copies, waits for them, and re-layouts  1.37 us (1%)
    pallas_call x1, Pallas kernels, shards(): pl.pallas_call(functools.partial(kernel, dims), out_shape=jax.ShapeDtypeS...  125 us

profile of v3, /device:TPU:103, one launch (start us, length us, event | category | flops | bytes accessed | tf_op | source)
XLA Modules:
  0.0 128.5 jit_solution(8018550116089624779)
XLA Ops:
  2.6 124.6 %shard_map.122 = f32[4,512]{1,0:T(4,128)} custom-call(bf16[2,512,1024]{2,1,0:T(8,128)(2,1)} %skew.1, f32[1024,1024]{1,0:T(8,128)} %gain_cross.1, f32[8,128]{1,0:T(8,128)} %bitcast.4, f32[1024,1024]{1,0:T(8,128)} %smooth_cross.1, f32[8,128]{1,0:T(8,128)} %bitcast.5, f32[8,128]{1,0:T(8,128)} %bitcast.6, f32[1,128]{1,0:T(1,128)} %obs_values.1, ...), custom_call_target="tpu_custom_call" | custom-call | tf_op jit(solution)/shard_map/pallas_call | solution.py:692
  127.1 1.4 %fusion = (f32[2,512]{1,0:T(2,128)}, f32[2,512]{1,0:T(2,128)}) fusion(f32[4,512]{1,0:T(4,128)} %shard_map.122), kind=kLoop, calls=%fused_computation | loop fusion | bytes 16384 | tf_op jit(solution)/shard_map/slice | solution.py:771

commit v4 on v3

--- a/solution.py
+++ b/solution.py
@@ -205,13 +205,13 @@
     slot = turn * 2 + core
     sensor_ids = lax.broadcasted_iota(jnp.int32, sensor_step.shape, 0) * LANES
     sensor_ids += lax.broadcasted_iota(jnp.int32, sensor_step.shape, 1)
-    found = jnp.where(sensor_ids == obs_sensor[0], sensor_step[...], 0).astype(F32)
+    found = jnp.where(sensor_ids == obs_sensor[...], sensor_step[...], 0).astype(F32)
     found = jnp.sum(jnp.sum(found, axis=0, keepdims=True), axis=1, keepdims=True)
     lane = lax.broadcasted_iota(jnp.int32, (1, LANES), 1)
     meta_row = jnp.where(
-        lane == 0, obs_prec[0], jnp.where(lane == 1, found, obs_block[0].astype(F32))
-    )
-    obs[slot, 0:1, :] = obs_prec[0] * obs_values[...]
+        lane == 0, obs_prec[...], jnp.where(lane == 1, found, obs_block[...].astype(F32))
+    )
+    obs[slot, 0:1, :] = obs_prec[...] * obs_values[...]
     obs[slot, 1:2, :] = meta_row
     ends = jnp.where(turn > 0, 2, 0) + jnp.where(sends_one, 2, 0)
     ends += jnp.where(sends_all, 2 * group, 0)
@@ -279,23 +279,21 @@
 
     strip = 256
 
-    def square_turn(block, carry):
-        rows = pl.ds(pl.multiple_of(block * strip, strip), strip)
-        value = dot3(a_high[rows, :], a_low[rows, :], a_high[...], a_low[...])
+    for block in range(width // strip):
+        first = block * strip
+        rows = slice(first, first + strip)
+        value = dot3(a_high[rows, :], a_low[rows, :], a_high[:, first:], a_low[:, first:])
+        tangent[rows, first:] = value
+        if first:
+            value = jnp.concatenate([tangent[:first, rows].T, value], axis=1)
         b_high[rows, :], b_low[rows, :] = split(value)
         a_value = a_high[rows, :].astype(F32) + a_low[rows, :].astype(F32)
-        w_value = 0.5 * eye_rows(block * strip, strip, width) + a_value / 6.0 + value / 24.0
+        w_value = 0.5 * eye_rows(first, strip, width) + a_value / 6.0 + value / 24.0
         w_high[rows, :], w_low[rows, :] = split(w_value)
-        return carry
-
-    lax.fori_loop(0, width // strip // 2, square_turn, 0)
-    for copy in ring_copies:
-        copy.wait()
-    ring_copies = obs_ring(1)
-    lax.fori_loop(width // strip // 2, width // strip, square_turn, 0)
-    for copy in ring_copies:
-        copy.wait()
-    ring_copies = obs_ring(2)
+        if block % 2 == 1:
+            for copy in ring_copies:
+                copy.wait()
+            ring_copies = obs_ring(1 + block // 2)
 
     def tangent_turn(block, carry):
         rows = pl.ds(pl.multiple_of(block * strip, strip), strip)
@@ -354,13 +352,13 @@
         return carry
 
     lax.fori_loop(0, width // strip, map_turn, 0)
+    map_copy(width // strip - 1, 0).start()
+    map_copy(width // strip - 1, 1).start()
 
     gain_tile = square(g_full)
     matvec_loop(gain_tile, [goal[0], goal[1]], [gain_goal.at[0], gain_goal.at[1]], blocks, blocks)
     for index in range(2):
         gain_goal[index] += gain_diag[...] * goal[index]
-    map_copy(width // strip - 1, 0).start()
-    map_copy(width // strip - 1, 1).start()
     for part in range(2):
         ref = (p_high, p_low)[part]
         whole = pltpu.make_async_remote_copy(
@@ -677,7 +675,6 @@
     blocks = width // LANES
     obs_total = lax.axis_size(("tm", "row"))
     vmem = pl.BlockSpec(memory_space=pltpu.VMEM)
-    smem = pl.BlockSpec(memory_space=pltpu.SMEM)
     hbm = pl.BlockSpec(memory_space=pltpu.HBM)
     chunks = width // 2 // CHUNK
     group = dims[2]
@@ -692,7 +689,7 @@
     result = pl.pallas_call(
         functools.partial(kernel, dims),
         out_shape=jax.ShapeDtypeStruct((4, width // 2), F32),
-        in_specs=[hbm, hbm, vmem, hbm, vmem, vmem, vmem, smem, smem, smem, vmem],
+        in_specs=[hbm, hbm, vmem, hbm] + [vmem] * 7,
         out_specs=vmem,
         scratch_shapes=[
             wide(BF16),
@@ -763,9 +760,9 @@
         smooth_diag.reshape(blocks, LANES),
         init_mean.reshape(blocks, LANES),
         obs_values,
-        obs_prec,
-        obs_sensor,
-        obs_block,
+        obs_prec.reshape(1, 1),
+        obs_sensor.reshape(1, 1),
+        obs_block.reshape(1, 1),
         sensor_step.reshape(-1, LANES),
     )
     return result[:2], result[2:]

time: 129 us -> 126 us (0.977)
  Pallas kernels: 125 us -> 122 us
    pallas_call x1, Pallas kernels: 125 us -> 122 us  [shards(): pl.pallas_call(functools.partial(kernel, dims), out_shape=jax.ShapeDtypeS...]
where the time goes in v4:
time: 126 us
  Pallas kernels  122 us (97%)
  between operations  2.58 us (2%)
  local copies, waits for them, and re-layouts  1.37 us (1%)
    pallas_call x1, Pallas kernels, shards(): pl.pallas_call(functools.partial(kernel, dims), out_shape=jax.ShapeDtypeS...  122 us

profile of v4, /device:TPU:103, one launch (start us, length us, event | category | flops | bytes accessed | tf_op | source)
XLA Modules:
  0.0 125.8 jit_solution(1869039034834595958)
XLA Ops:
  2.6 121.8 %shard_map.122 = f32[4,512]{1,0:T(4,128)} custom-call(bf16[2,512,1024]{2,1,0:T(8,128)(2,1)} %skew.1, f32[1024,1024]{1,0:T(8,128)} %gain_cross.1, f32[8,128]{1,0:T(8,128)} %bitcast.10, f32[1024,1024]{1,0:T(8,128)} %smooth_cross.1, f32[8,128]{1,0:T(8,128)} %bitcast.11, f32[8,128]{1,0:T(8,128)} %bitcast.12, f32[1,128]{1,0:T(1,128)} %obs_values.1, ...), custom_call_target="tpu_custom_call" | custom-call | tf_op jit(solution)/shard_map/pallas_call | solution.py:689
  124.4 1.4 %fusion = (f32[2,512]{1,0:T(2,128)}, f32[2,512]{1,0:T(2,128)}) fusion(f32[4,512]{1,0:T(4,128)} %shard_map.122), kind=kLoop, calls=%fused_computation | loop fusion | bytes 16384 | tf_op jit(solution)/shard_map/slice | solution.py:768

commit v5 on v4

--- a/solution.py
+++ b/solution.py
@@ -15,7 +15,7 @@
 VMEM_BYTES = 67043328
 LEVELS = 32767.0
 CHUNK = 64
-UNROLL = 4
+UNROLL = 8
 dot = functools.partial(jnp.dot, preferred_element_type=F32)
 
 
@@ -48,15 +48,17 @@
 
 
 def matvec_loop(tile, vectors, outs, out_blocks, groups):
+    unroll = min(UNROLL, out_blocks)
+
     def block_turn(turn, carry):
-        first = turn * UNROLL
-        found = matvec(lambda block, group: tile(first + block, group), vectors, UNROLL, groups)
+        first = turn * unroll
+        found = matvec(lambda block, group: tile(first + block, group), vectors, unroll, groups)
         for index, rows in enumerate(found):
-            for block in range(UNROLL):
+            for block in range(unroll):
                 outs[index][pl.ds(first + block, 1), :] = rows[block : block + 1]
         return carry
 
-    lax.fori_loop(0, out_blocks // UNROLL, block_turn, 0)
+    lax.fori_loop(0, out_blocks // unroll, block_turn, 0)
 
 
 def square(ref):
@@ -295,15 +297,17 @@
                 copy.wait()
             ring_copies = obs_ring(1 + block // 2)
 
+    broad = 512
+
     def tangent_turn(block, carry):
-        rows = pl.ds(pl.multiple_of(block * strip, strip), strip)
+        rows = pl.ds(pl.multiple_of(block * broad, broad), broad)
         value = dot3(b_high[rows, :], b_low[rows, :], w_high[...], w_low[...])
         a_value = a_high[rows, :].astype(F32) + a_low[rows, :].astype(F32)
-        value = eye_rows(block * strip, strip, width) + a_value + value
+        value = eye_rows(block * broad, broad, width) + a_value + value
         tangent[rows, :] = value
         return carry
 
-    lax.fori_loop(0, width // strip, tangent_turn, 0)
+    lax.fori_loop(0, width // broad, tangent_turn, 0)
     for copy in ring_copies:
         copy.wait()
 
@@ -525,7 +529,7 @@
                 dst_ref=arrived.at[core],
                 send_sem=chain_send.at[2 * step + target],
                 recv_sem=chain_recv,
-                **at(turn + 1 + step, target),
+                **at(turn + 1 + step, lax.rem(core + target, 2)),
             )
             for step in order
             for target in range(2)

time: 126 us -> 125 us (level)
  no operation moved by 1% of the time
where the time goes in v5:
time: 125 us
  Pallas kernels  121 us (97%)
  between operations  2.58 us (2%)
  local copies, waits for them, and re-layouts  1.37 us (1%)
    pallas_call x1, Pallas kernels, shards(): pl.pallas_call(functools.partial(kernel, dims), out_shape=jax.ShapeDtypeS...  121 us

profile of v5, /device:TPU:103, one launch (start us, length us, event | category | flops | bytes accessed | tf_op | source)
XLA Modules:
  0.0 125.2 jit_solution(1174532524724587278)
XLA Ops:
  2.6 121.2 %shard_map.122 = f32[4,512]{1,0:T(4,128)} custom-call(bf16[2,512,1024]{2,1,0:T(8,128)(2,1)} %skew.1, f32[1024,1024]{1,0:T(8,128)} %gain_cross.1, f32[8,128]{1,0:T(8,128)} %bitcast.10, f32[1024,1024]{1,0:T(8,128)} %smooth_cross.1, f32[8,128]{1,0:T(8,128)} %bitcast.11, f32[8,128]{1,0:T(8,128)} %bitcast.12, f32[1,128]{1,0:T(1,128)} %obs_values.1, ...), custom_call_target="tpu_custom_call" | custom-call | tf_op jit(solution)/shard_map/pallas_call | solution.py:693
  123.8 1.4 %fusion = (f32[2,512]{1,0:T(2,128)}, f32[2,512]{1,0:T(2,128)}) fusion(f32[4,512]{1,0:T(4,128)} %shard_map.122), kind=kLoop, calls=%fused_computation | loop fusion | bytes 16384 | tf_op jit(solution)/shard_map/slice | solution.py:772
